TPU v7x, 32 devices: a whole 2x2x4 slice. The times are simulated.
32 devices in a mesh: dp: 8 (over y, x, core), mp: 4 (over z).
Axes of the slice: x: 2, y: 2, z: 4, core: 2. Of those that a mesh axis runs over, the one named last changes fastest.
Arguments:
- tokens_in: bfloat16 [8192, 2048], P('dp'), may hold values from -6 to 6
- cotangent: bfloat16 [8192, 2048], P('dp'), may hold values from -6 to 6
- seq_lengths: int32 [8, 4], P('dp'), may hold values from 0 to 512, as said below
- qkv_weight: bfloat16 [2, 2048, 6144], P(None, 'dp', 'mp'), may hold values from -0.125 to 0.125
- dense_weight: bfloat16 [2, 2048, 2048], P(None, 'mp', 'dp'), may hold values from -0.5 to 0.5
- up_weight: bfloat16 [2, 2048, 8192], P(None, 'dp', 'mp'), may hold values from -0.125 to 0.125
- down_weight: bfloat16 [2, 8192, 2048], P(None, 'mp', 'dp'), may hold values from -0.0625 to 0.0625
- qkv_bias: bfloat16 [2, 48, 128], P(None, 'mp', 'dp'), may hold values from -3 to 3
- up_bias: bfloat16 [2, 64, 128], P(None, 'mp', 'dp'), may hold values from -3 to 3
- vectors: bfloat16 [2, 6, 2048], P(None, None, 'dp')
- qkv_weight_first: float32 [2, 2048, 6144], P(None, 'dp', 'mp'), may hold values from -96 to 96
- dense_weight_first: float32 [2, 2048, 2048], P(None, 'mp', 'dp'), may hold values from -48 to 48
- up_weight_first: float32 [2, 2048, 8192], P(None, 'dp', 'mp'), may hold values from -16 to 16
- down_weight_first: float32 [2, 8192, 2048], P(None, 'mp', 'dp'), may hold values from -40 to 40
- qkv_bias_first: float32 [2, 48, 128], P(None, 'mp', 'dp'), may hold values from -128 to 128
- up_bias_first: float32 [2, 64, 128], P(None, 'mp', 'dp'), may hold values from -16 to 16
- vectors_first: float32 [2, 6, 2048], P(None, None, 'dp'), may hold values from -128 to 128
- qkv_weight_second: float32 [2, 2048, 6144], P(None, 'dp', 'mp'), may hold values from 1720.32 to 6799.36
- dense_weight_second: float32 [2, 2048, 2048], P(None, 'mp', 'dp'), may hold values from 450.56 to 1802.24
- up_weight_second: float32 [2, 2048, 8192], P(None, 'dp', 'mp'), may hold values from 61.44 to 245.76
- down_weight_second: float32 [2, 8192, 2048], P(None, 'mp', 'dp'), may hold values from 327.68 to 1310.72
- qkv_bias_second: float32 [2, 48, 128], P(None, 'mp', 'dp'), may hold values from 4096 to 16384
- up_bias_second: float32 [2, 64, 128], P(None, 'mp', 'dp'), may hold values from 39.3216 to 155.648
- vectors_second: float32 [2, 6, 2048], P(None, None, 'dp'), may hold values from 2293.76 to 9256.96
Outputs:
- block_output: bfloat16 [8192, 2048], P('dp')
- input_grad: float32 [8192, 2048], P('dp')
- qkv_weight_grad: float32 [2, 2048, 6144], P(None, 'dp', 'mp')
- qkv_weight_first_new: float32 [2, 2048, 6144], P(None, 'dp', 'mp')
- qkv_weight_second_new: float32 [2, 2048, 6144], P(None, 'dp', 'mp')
- qkv_weight_step: float32 [2, 2048, 6144], P(None, 'dp', 'mp')
- dense_weight_grad: float32 [2, 2048, 2048], P(None, 'mp', 'dp')
- dense_weight_first_new: float32 [2, 2048, 2048], P(None, 'mp', 'dp')
- dense_weight_second_new: float32 [2, 2048, 2048], P(None, 'mp', 'dp')
- dense_weight_step: float32 [2, 2048, 2048], P(None, 'mp', 'dp')
- up_weight_grad: float32 [2, 2048, 8192], P(None, 'dp', 'mp')
- up_weight_first_new: float32 [2, 2048, 8192], P(None, 'dp', 'mp')
- up_weight_second_new: float32 [2, 2048, 8192], P(None, 'dp', 'mp')
- up_weight_step: float32 [2, 2048, 8192], P(None, 'dp', 'mp')
- down_weight_grad: float32 [2, 8192, 2048], P(None, 'mp', 'dp')
- down_weight_first_new: float32 [2, 8192, 2048], P(None, 'mp', 'dp')
- down_weight_second_new: float32 [2, 8192, 2048], P(None, 'mp', 'dp')
- down_weight_step: float32 [2, 8192, 2048], P(None, 'mp', 'dp')
- qkv_bias_grad: float32 [2, 48, 128], P(None, 'mp', 'dp')
- qkv_bias_first_new: float32 [2, 48, 128], P(None, 'mp', 'dp')
- qkv_bias_second_new: float32 [2, 48, 128], P(None, 'mp', 'dp')
- qkv_bias_step: float32 [2, 48, 128], P(None, 'mp', 'dp')
- up_bias_grad: float32 [2, 64, 128], P(None, 'mp', 'dp')
- up_bias_first_new: float32 [2, 64, 128], P(None, 'mp', 'dp')
- up_bias_second_new: float32 [2, 64, 128], P(None, 'mp', 'dp')
- up_bias_step: float32 [2, 64, 128], P(None, 'mp', 'dp')
- vectors_grad: float32 [2, 6, 2048], P(None, None, 'dp')
- updated_vector_first_moment: float32 [2, 6, 2048], P(None, None, 'dp')
- vectors_second_new: float32 [2, 6, 2048], P(None, None, 'dp')
- vectors_step: float32 [2, 6, 2048], P(None, None, 'dp')
Inputs may be any that keep to these rules, and one draw needn't show every extreme that they name: `seq_lengths`: A zero marks an empty slot; the lengths of one index of dp sum to at most 1024, and in every draw some index of dp sums to exactly 1024 with sequences of 512; any other length lies between 64 and 512.
All inputs are finite; a program needn't handle non-finite values.
Results may differ from a plain program's by a relative error of at most 0.012.
Values may be sent and summed in bfloat16 or wider, within the bound.
A program may use at most 384 MiB of HBM per device.

v0:
```python
import jax
import jax.numpy as jnp
from jax import lax
from jax.sharding import PartitionSpec as P

HD = 256
ROT = 64
LAYERS = 2
MAXLEN = 512
ADAM_STEP = 10
norm_eps = 1e-05
beta_one = 0.9
beta_two = 0.95
adam_eps = 1e-08
rate = 0.02
decay = 0.01
masked_score = -1e30


def layout(lengths_row, rows):
    slots = lengths_row.shape[0]
    ends = jnp.cumsum(lengths_row)
    starts = ends - lengths_row
    index = jnp.arange(rows, dtype=jnp.int32)
    inside = (index[:, None] >= starts[None, :]) & (index[:, None] < ends[None, :])
    valid = jnp.any(inside, axis=1)
    number = jnp.arange(slots, dtype=jnp.int32)
    slot = jnp.sum(jnp.where(inside, number[None, :], 0), axis=1)
    first = jnp.sum(jnp.where(inside, starts[None, :], 0), axis=1)
    segment = jnp.where(valid, slot, slots + index)
    position = index - first
    return (segment, position, valid)


def rotary_tables(position):
    half = ROT // 2
    freq = 10000.0 ** (-(jnp.arange(half, dtype=jnp.float32) * 2.0) / ROT)
    angle = position.astype(jnp.float32)[:, None] * freq[None, :]
    return (jnp.cos(angle), jnp.sin(angle))


def rotate(values, cosine, sine):
    half = cosine.shape[1]
    first = values[..., :half]
    second = values[..., half : 2 * half]
    rest = values[..., 2 * half :]
    cfac = cosine[:, None, :]
    sfac = sine[:, None, :]
    return jnp.concatenate(
        [first * cfac - second * sfac, second * cfac + first * sfac, rest], axis=-1
    )


def apply_layer_norm(residual_stream):
    centre = jnp.mean(residual_stream, axis=1, keepdims=True)
    centred = residual_stream - centre
    spread = jnp.mean(centred * centred, axis=1, keepdims=True)
    return centred * lax.rsqrt(spread + norm_eps)


def norm_pair(residual_stream, model_parameters):
    normalized_input_rows = apply_layer_norm(residual_stream)
    return (
        normalized_input_rows * model_parameters[0] + model_parameters[1],
        normalized_input_rows * model_parameters[2] + model_parameters[3],
    )


def gelu_exact(values):
    return jax.nn.gelu(values, approximate=False)


def padded_inputs(keys, values, segment):
    block = MAXLEN
    rows, heads, width = keys.shape
    zeros = jnp.zeros((block, heads, width), keys.dtype)
    keys_pad = jnp.concatenate([zeros, keys], axis=0)
    values_pad = jnp.concatenate([zeros, values], axis=0)
    seg_pad = jnp.concatenate([jnp.full((block,), -1, jnp.int32), segment])
    padded_index_rows = jnp.arange(-block, rows, dtype=jnp.int32)
    return (keys_pad, values_pad, seg_pad, padded_index_rows)


def window(query, keys_pad, values_pad, seg_pad, padded_index_rows, segment, number):
    block = MAXLEN
    start = number * block
    q_blk = lax.dynamic_slice_in_dim(query, start, block, 0)
    k_win = lax.dynamic_slice_in_dim(keys_pad, start, 2 * block, 0)
    v_win = lax.dynamic_slice_in_dim(values_pad, start, 2 * block, 0)
    seg_q = lax.dynamic_slice_in_dim(segment, start, block, 0)
    seg_k = lax.dynamic_slice_in_dim(seg_pad, start, 2 * block, 0)
    idx_q = start + jnp.arange(block, dtype=jnp.int32)
    idx_k = lax.dynamic_slice_in_dim(padded_index_rows, start, 2 * block, 0)
    allowed = (seg_q[:, None] == seg_k[None, :]) & (idx_k[None, :] <= idx_q[:, None])
    scores = jnp.einsum("qhd,khd->hqk", q_blk, k_win, preferred_element_type=jnp.float32) * HD ** (
        -0.5
    )
    scores = jnp.where(allowed[None], scores, masked_score)
    return (start, q_blk, k_win, v_win, scores)


def attention_forward(query, keys, values, segment):
    rows, heads, width = query.shape
    count = rows // MAXLEN
    keys_pad, values_pad, seg_pad, padded_index_rows = padded_inputs(keys, values, segment)

    def one_block(number):
        start, q_blk, k_win, v_win, scores = window(
            query, keys_pad, values_pad, seg_pad, padded_index_rows, segment, number
        )
        top = jnp.max(scores, axis=2, keepdims=True)
        expo = jnp.exp(scores - top)
        total = jnp.sum(expo, axis=2, keepdims=True)
        prob = (expo / total).astype(jnp.bfloat16)
        context = jnp.einsum("hqk,khd->qhd", prob, v_win, preferred_element_type=jnp.float32)
        return (context.astype(jnp.bfloat16), (top + jnp.log(total))[:, :, 0])

    context, logsum = lax.map(one_block, jnp.arange(count, dtype=jnp.int32))
    return (context.reshape(rows, heads * width), logsum)


def attention_backward(query, keys, values, d_context, logsum, segment):
    rows, heads, width = query.shape
    block = MAXLEN
    count = rows // block
    keys_pad, values_pad, seg_pad, padded_index_rows = padded_inputs(keys, values, segment)

    def one_block(carry, inputs):
        dk_acc, dv_acc = carry
        number, lse_blk = inputs
        start, q_blk, k_win, v_win, scores = window(
            query, keys_pad, values_pad, seg_pad, padded_index_rows, segment, number
        )
        do_blk = lax.dynamic_slice_in_dim(d_context, start, block, 0)
        prob = jnp.exp(scores - lse_blk[:, :, None])
        d_prob = jnp.einsum("qhd,khd->hqk", do_blk, v_win, preferred_element_type=jnp.float32)
        delta = jnp.sum(prob * d_prob, axis=2, keepdims=True)
        d_score = (prob * (d_prob - delta)).astype(jnp.bfloat16)
        d_query = jnp.einsum(
            "hqk,khd->qhd", d_score, k_win, preferred_element_type=jnp.float32
        ) * HD ** (-0.5)
        d_keys = jnp.einsum(
            "hqk,qhd->khd", d_score, q_blk, preferred_element_type=jnp.float32
        ) * HD ** (-0.5)
        d_values = jnp.einsum(
            "hqk,qhd->khd", prob.astype(jnp.bfloat16), do_blk, preferred_element_type=jnp.float32
        )
        dk_acc = lax.dynamic_update_slice_in_dim(
            dk_acc, lax.dynamic_slice_in_dim(dk_acc, start, 2 * block, 0) + d_keys, start, 0
        )
        dv_acc = lax.dynamic_update_slice_in_dim(
            dv_acc, lax.dynamic_slice_in_dim(dv_acc, start, 2 * block, 0) + d_values, start, 0
        )
        return ((dk_acc, dv_acc), d_query)

    empty = jnp.zeros((rows + block, heads, width), jnp.float32)
    (dk_acc, dv_acc), d_query = lax.scan(
        one_block, (empty, empty), (jnp.arange(count, dtype=jnp.int32), logsum)
    )
    return (d_query.reshape(rows, heads, width), dk_acc[block:], dv_acc[block:])


def fetch(shards, layer):
    return (
        lax.all_gather(shards[0][layer], "dp", axis=0, tiled=True),
        lax.all_gather(shards[1][layer], "dp", axis=1, tiled=True),
        lax.all_gather(shards[2][layer], "dp", axis=0, tiled=True),
        lax.all_gather(shards[3][layer], "dp", axis=1, tiled=True),
        lax.all_gather(shards[4][layer], "dp", axis=1, tiled=True),
        lax.all_gather(shards[5][layer], "dp", axis=1, tiled=True),
        lax.all_gather(shards[6][layer], "dp", axis=1, tiled=True),
    )


def reduce_grads(grads):
    return (
        lax.psum_scatter(grads[0], "dp", scatter_dimension=1, tiled=True),
        lax.psum_scatter(grads[1], "dp", scatter_dimension=2, tiled=True),
        lax.psum_scatter(grads[2], "dp", scatter_dimension=1, tiled=True),
        lax.psum_scatter(grads[3], "dp", scatter_dimension=2, tiled=True),
        lax.psum_scatter(grads[4], "dp", scatter_dimension=2, tiled=True),
        lax.psum_scatter(grads[5], "dp", scatter_dimension=2, tiled=True),
        lax.psum_scatter(grads[6], "dp", scatter_dimension=2, tiled=True),
    )


def layer_forward(residual_stream, weights, segment, cosine, sine):
    qkv_w, dense_w, up_w, down_w, qkv_b, up_b, vec = weights
    heads = qkv_w.shape[1] // (3 * HD)
    vec_wide = vec.astype(jnp.float32)
    first_branch_input, second_in = norm_pair(residual_stream, vec_wide[:4])
    first_branch_input = first_branch_input.astype(jnp.bfloat16)
    second_in = second_in.astype(jnp.bfloat16)
    rows = first_branch_input.shape[0]
    mixed = jnp.dot(first_branch_input, qkv_w, preferred_element_type=jnp.float32) + qkv_b.reshape(
        -1
    ).astype(jnp.float32)
    mixed = mixed.reshape(rows, heads, 3, HD)
    query = rotate(mixed[:, :, 0], cosine, sine).astype(jnp.bfloat16)
    keys = rotate(mixed[:, :, 1], cosine, sine).astype(jnp.bfloat16)
    values = mixed[:, :, 2].astype(jnp.bfloat16)
    context, logsum = attention_forward(query, keys, values, segment)
    hidden = jnp.dot(second_in, up_w, preferred_element_type=jnp.float32) + up_b.reshape(-1).astype(
        jnp.float32
    )
    active = gelu_exact(hidden).astype(jnp.bfloat16)
    branch = jnp.dot(context, dense_w, preferred_element_type=jnp.float32) + jnp.dot(
        active, down_w, preferred_element_type=jnp.float32
    )
    branch = lax.psum(branch, "mp")
    result = residual_stream + branch + vec_wide[4] + vec_wide[5]
    return (
        result,
        (first_branch_input, second_in, query, keys, values, context, logsum, hidden, active),
    )


def layer_backward(residual_stream, weights, kept, grad_out, segment, cosine, sine):
    qkv_w, dense_w, up_w, down_w, qkv_b, up_b, vec = weights
    first_branch_input, second_in, query, keys, values, context, logsum, hidden, active = kept
    rows, heads = (query.shape[0], query.shape[1])
    grad_low = grad_out.astype(jnp.bfloat16)
    d_dense = jnp.dot(context.T, grad_low, preferred_element_type=jnp.float32)
    d_down = jnp.dot(active.T, grad_low, preferred_element_type=jnp.float32)
    d_context = (
        jnp.dot(grad_low, dense_w.T, preferred_element_type=jnp.float32)
        .astype(jnp.bfloat16)
        .reshape(rows, heads, HD)
    )
    d_active = jnp.dot(grad_low, down_w.T, preferred_element_type=jnp.float32)
    d_hidden = jax.vjp(gelu_exact, hidden)[1](d_active)[0].astype(jnp.bfloat16)
    d_up = jnp.dot(second_in.T, d_hidden, preferred_element_type=jnp.float32)
    d_up_bias = jnp.sum(d_hidden.astype(jnp.float32), axis=0)
    d_second = jnp.dot(d_hidden, up_w.T, preferred_element_type=jnp.float32)
    d_query, d_keys, d_values = attention_backward(query, keys, values, d_context, logsum, segment)
    d_mixed = jnp.stack(
        [rotate(d_query, cosine, -sine), rotate(d_keys, cosine, -sine), d_values], axis=2
    )
    d_mixed = d_mixed.reshape(rows, heads * 3 * HD).astype(jnp.bfloat16)
    d_qkv = jnp.dot(first_branch_input.T, d_mixed, preferred_element_type=jnp.float32)
    d_qkv_bias = jnp.sum(d_mixed.astype(jnp.float32), axis=0)
    d_first = jnp.dot(d_mixed, qkv_w.T, preferred_element_type=jnp.float32)
    vec_wide = vec.astype(jnp.float32)
    pullback = jax.vjp(norm_pair, residual_stream, vec_wide[:4])[1]
    d_resid, d_norm = pullback((d_first, d_second))
    d_resid, d_norm = lax.psum((d_resid, d_norm), "mp")
    d_out_bias = jnp.sum(grad_out, axis=0)
    d_vec = jnp.concatenate([d_norm, d_out_bias[None], d_out_bias[None]], axis=0)
    grads = (
        d_qkv,
        d_dense,
        d_up,
        d_down,
        d_qkv_bias.reshape(qkv_b.shape[0], -1),
        d_up_bias.reshape(up_b.shape[0], -1),
        d_vec,
    )
    return (grad_out + d_resid, grads)


def adam(weight, grad, first, second):
    first_new = beta_one * first + (1.0 - beta_one) * grad
    second_new = beta_two * second + (1.0 - beta_two) * grad * grad
    mean_hat = first_new / (1.0 - beta_one**ADAM_STEP)
    square_hat = second_new / (1.0 - beta_two**ADAM_STEP)
    old = weight.astype(jnp.float32)
    new_weight = old - rate * (mean_hat / (jnp.sqrt(square_hat) + adam_eps) + decay * old)
    return (grad, first_new, second_new, new_weight - old)


def body(
    tokens_in,
    cotangent,
    seq_lengths,
    qkv_weight,
    dense_weight,
    up_weight,
    down_weight,
    qkv_bias,
    up_bias,
    vectors,
    qkv_weight_first,
    dense_weight_first,
    up_weight_first,
    down_weight_first,
    qkv_bias_first,
    up_bias_first,
    vectors_first,
    qkv_weight_second,
    dense_weight_second,
    up_weight_second,
    down_weight_second,
    qkv_bias_second,
    up_bias_second,
    vectors_second,
):
    rows = tokens_in.shape[0]
    segment, position, valid = layout(seq_lengths[0], rows)
    cosine, sine = rotary_tables(position)
    shards = (qkv_weight, dense_weight, up_weight, down_weight, qkv_bias, up_bias, vectors)
    firsts = (
        qkv_weight_first,
        dense_weight_first,
        up_weight_first,
        down_weight_first,
        qkv_bias_first,
        up_bias_first,
        vectors_first,
    )
    seconds = (
        qkv_weight_second,
        dense_weight_second,
        up_weight_second,
        down_weight_second,
        qkv_bias_second,
        up_bias_second,
        vectors_second,
    )
    live = valid.astype(jnp.float32)[:, None]
    residual_stream = tokens_in.astype(jnp.float32)
    inputs, saved, fetched = ([], [], [])
    for layer in range(LAYERS):
        weights = fetch(shards, layer)
        inputs.append(residual_stream)
        residual_stream, kept = layer_forward(residual_stream, weights, segment, cosine, sine)
        saved.append(kept)
        fetched.append(weights)
    output = (residual_stream * live).astype(jnp.bfloat16)
    grad = cotangent.astype(jnp.float32) * live
    per_layer = [None] * LAYERS
    for layer in reversed(range(LAYERS)):
        weights = fetch(shards, layer)
        grad, grads = layer_backward(
            inputs[layer], weights, saved[layer], grad, segment, cosine, sine
        )
        per_layer[layer] = reduce_grads(tuple((item[None] for item in grads)))
    owned = tuple(
        (
            jnp.concatenate([per_layer[layer][slot] for layer in range(LAYERS)], axis=0)
            for slot in range(7)
        )
    )
    outs = [output, grad]
    for weight, summed, first, second in zip(shards, owned, firsts, seconds):
        outs.extend(adam(weight, summed, first, second))
    return tuple(outs)


def solution(mesh):
    placed = (
        P("dp", None),
        P("dp", None),
        P("dp", None),
        P(None, "dp", "mp"),
        P(None, "mp", "dp"),
        P(None, "dp", "mp"),
        P(None, "mp", "dp"),
        P(None, "mp", "dp"),
        P(None, "mp", "dp"),
        P(None, None, "dp"),
        P(None, "dp", "mp"),
        P(None, "mp", "dp"),
        P(None, "dp", "mp"),
        P(None, "mp", "dp"),
        P(None, "mp", "dp"),
        P(None, "mp", "dp"),
        P(None, None, "dp"),
        P(None, "dp", "mp"),
        P(None, "mp", "dp"),
        P(None, "dp", "mp"),
        P(None, "mp", "dp"),
        P(None, "mp", "dp"),
        P(None, "mp", "dp"),
        P(None, None, "dp"),
    )
    return jax.shard_map(
        body,
        mesh=mesh,
        in_specs=placed,
        out_specs=(
            P("dp", None),
            P("dp", None),
            P(None, "dp", "mp"),
            P(None, "dp", "mp"),
            P(None, "dp", "mp"),
            P(None, "dp", "mp"),
            P(None, "mp", "dp"),
            P(None, "mp", "dp"),
            P(None, "mp", "dp"),
            P(None, "mp", "dp"),
            P(None, "dp", "mp"),
            P(None, "dp", "mp"),
            P(None, "dp", "mp"),
            P(None, "dp", "mp"),
            P(None, "mp", "dp"),
            P(None, "mp", "dp"),
            P(None, "mp", "dp"),
            P(None, "mp", "dp"),
            P(None, "mp", "dp"),
            P(None, "mp", "dp"),
            P(None, "mp", "dp"),
            P(None, "mp", "dp"),
            P(None, "mp", "dp"),
            P(None, "mp", "dp"),
            P(None, "mp", "dp"),
            P(None, "mp", "dp"),
            P(None, None, "dp"),
            P(None, None, "dp"),
            P(None, None, "dp"),
            P(None, None, "dp"),
        ),
        check_vma=False,
    )
```

profile of v0, /device:TPU:0, one launch (start us, length us, event | category | flops | bytes accessed | tf_op | source)
XLA Modules:
  0.0 2900.1 jit_solution(7552632364524277170)
XLA Ops:
  115.0 31.7 %all-gather.27.cloned.1.call-done = bf16[1,2048,2048]{2,1,0:T(8,128)(2,1)} async-done(((bf16[1,256,2048]{2,1,0:T(8,128)(2,1)}), bf16[1,2048,2048]{2,1,0:T(8,128)(2,1)}) %all-gather.27.cloned.1.call-update) | async-done | bytes 8388624 | tf_op jit(solution)/shard_map/all_gather | solution.py:167
  146.7 33.9 %multiply_convert_fusion.4 = (bf16[1024,2048]{1,0:T(8,128)(2,1)}, f32[1024,2048]{1,0:T(8,128)}, f32[1024,2048]{1,0:T(8,128)}) fusion(f32[2048]{0:T(1024)S(1)} %bitcast_convert_fusion.2, bf16[1,2048,2048]{2,1,0:T(8,128)(2,1)} %all-gather.27.cloned.1.call-done, bf16[1024,2048]{1,0:T(8,128)(2,1)} %param.32, f32[2048]{0:T(1024)S(1)} %bitcast.349, ...), kind=kOutput, calls=%fused_computation.189 | convolution fusion | flops 8740929536 | bytes 33587200 | tf_op jit(solution)/shard_map/dot_general | solution.py:203
  180.5 24.4 all-gather.29.cloned.1.call-done
  257.5 272.0 %all-reduce.20.cloned.1.call-done = f32[1024,2048]{1,0:T(8,128)} async-done(((f32[1024,2048]{1,0:T(8,128)}), f32[1024,2048]{1,0:T(8,128)}) %all-reduce.20.cloned.1.call-update) | async-done | bytes 8388624 | tf_op jit(solution)/shard_map/psum | solution.py:210
  539.5 37.0 %all-gather.31.cloned.1.call-done = bf16[1,2048,1536]{2,1,0:T(8,128)(2,1)} async-done(((bf16[1,256,1536]{2,1,0:T(8,128)(2,1)}), bf16[1,2048,1536]{2,1,0:T(8,128)(2,1)}) %all-gather.31.cloned.1.call-update) | async-done | bytes 6291472 | tf_op jit(solution)/shard_map/all_gather | solution.py:165
  630.0 72.7 %while.54 = (s32[]{:T(128)}, f32[1536,2,256]{0,2,1:T(8,128)}, f32[1536,2,256]{0,2,1:T(8,128)}, f32[2,512,2,256]{1,0,3,2:T(2,128)}, s32[2]{0:T(128)S(1)}, /*index...) while((s32[]{:T(128)}, f32[1536,2,256]{0,2,1:T(8,128)}, ...), condition=%wide.region_20.21_spmd, body=%wide.region_18.20_spmd.sunk | while | flops 2703490560 | bytes 109115848 | solution.py:157
  723.4 33.7 %multiply_convert_fusion.3 = (bf16[1024,2048]{1,0:T(8,128)(2,1)}, f32[1024,2048]{1,0:T(8,128)}, f32[1024,2048]{1,0:T(8,128)}) fusion(f32[2048]{0:T(1024)S(1)} %copy-done.109, bf16[1,2048,2048]{2,1,0:T(8,128)(2,1)} %all-gather.35.cloned.1.call-done, f32[1024,2048]{1,0:T(8,128)} %copy-done.1, f32[2048]{0:T(1024)S(1)} %bitcast.353, f32[2048]{0:T(1024)S(1)} %bitcast.337, ...), kind=kOutput, calls=%fused_computation.173 | convolution fusion | flops 8738832384 | bytes 37781504 | tf_op jit(solution)/shard_map/dot_general | solution.py:203
  757.2 23.6 convert_reduce_fusion.1
  780.8 22.2 multiply_reduce_fusion.3
  835.6 272.7 %all-reduce.22.cloned.1.call-done = f32[1024,2048]{1,0:T(8,128)} async-done(((f32[1024,2048]{1,0:T(8,128)}), f32[1024,2048]{1,0:T(8,128)}) %all-reduce.22.cloned.1.call-update) | async-done | bytes 8388624 | tf_op jit(solution)/shard_map/psum | solution.py:246
  1121.3 70.4 %while.55 = (s32[]{:T(128)}, f32[1536,2,256]{0,2,1:T(8,128)}, f32[1536,2,256]{2,0,1:T(8,128)}, f32[2,512,2,256]{3,1,0,2:T(8,128)}, s32[2]{0:T(128)S(1)}, /*index...) while((s32[]{:T(128)}, f32[1536,2,256]{0,2,1:T(8,128)}, ...), condition=%wide.region_26.27_spmd, body=%wide.region_24.26_spmd.sunk | while | flops 2703490560 | bytes 98629992 | solution.py:157
  1298.7 542.4 %all-reduce.26.cloned.1.call-done = (f32[1024,2048]{1,0:T(8,128)}, f32[1024,2048]{1,0:T(8,128)}) async-done(((f32[1024,2048]{1,0:T(8,128)}, f32[1024,2048]{1,0:T(8,128)}), (f32[1024,2048]{1,0:T(8,128)}, f32[1024,2048]{1,0:T(8,128)})) %all-reduce.26.cloned.1.call-update) | async-done | bytes 16777232 | tf_op jit(solution)/shard_map/psum | solution.py:210
  1841.1 19.8 fusion.117
  1990.7 33.4 %reduce-scatter.47.cloned.1.call-done = f32[16,16]{1,0:T(8,128)} async-done(((f32[128,16]{1,0:T(8,128)}), f32[16,16]{1,0:T(8,128)}) %reduce-scatter.47.cloned.1.call-update) | async-done | bytes 1040
  2025.6 54.1 %reduce-scatter.27.cloned.1.call-done = f32[1,512,256]{2,1,0:T(8,128)} async-done(((f32[1,512,2048]{2,1,0:T(8,128)}), f32[1,512,256]{2,1,0:T(8,128)}) %reduce-scatter.27.cloned.1.call-update) | async-done | bytes 524304 | tf_op jit(solution)/shard_map/reduce_scatter | solution.py:178
  2080.8 54.0 %reduce-scatter.29.cloned.1.call-done = f32[1,512,256]{2,1,0:T(8,128)} async-done(((f32[1,512,2048]{2,1,0:T(8,128)}), f32[1,512,256]{2,1,0:T(8,128)}) %reduce-scatter.29.cloned.1.call-update) | async-done | bytes 524304 | tf_op jit(solution)/shard_map/reduce_scatter | solution.py:178
  2139.7 32.2 %reduce-scatter.39.cloned.1.call-done = f32[1,6,256]{2,1,0:T(8,128)} async-done(((f32[1,6,2048]{2,1,0:T(8,128)}), f32[1,6,256]{2,1,0:T(8,128)}) %reduce-scatter.39.cloned.1.call-update) | async-done | bytes 6160 | tf_op jit(solution)/shard_map/reduce_scatter | solution.py:183
  2172.6 36.0 %reduce-scatter.41.cloned.1.call-done = f32[1,6,256]{2,1,0:T(8,128)} async-done(((f32[1,6,2048]{2,1,0:T(8,128)}), f32[1,6,256]{2,1,0:T(8,128)}) %reduce-scatter.41.cloned.1.call-update) | async-done | bytes 6160 | tf_op jit(solution)/shard_map/reduce_scatter | solution.py:183
  2211.8 93.2 %reduce-scatter.23.cloned.1.call-done = f32[1,256,1536]{2,1,0:T(8,128)} async-done(((f32[1,2048,1536]{2,1,0:T(8,128)}), f32[1,256,1536]{2,1,0:T(8,128)}) %reduce-scatter.23.cloned.1.call-update) | async-done | bytes 1572880 | tf_op jit(solution)/shard_map/reduce_scatter | solution.py:177
  2306.5 94.8 %reduce-scatter.25.cloned.1.call-done = f32[1,256,1536]{2,1,0:T(8,128)} async-done(((f32[1,2048,1536]{2,1,0:T(8,128)}), f32[1,256,1536]{2,1,0:T(8,128)}) %reduce-scatter.25.cloned.1.call-update) | async-done | bytes 1572880 | tf_op jit(solution)/shard_map/reduce_scatter | solution.py:177
  2410.8 110.5 %reduce-scatter.31.cloned.1.call-done = f32[1,256,2048]{2,1,0:T(8,128)} async-done(((f32[1,2048,2048]{2,1,0:T(8,128)}), f32[1,256,2048]{2,1,0:T(8,128)}) %reduce-scatter.31.cloned.1.call-update) | async-done | bytes 2097168 | tf_op jit(solution)/shard_map/reduce_scatter | solution.py:179
  2524.4 116.7 %reduce-scatter.35.cloned.1.call-done = f32[1,2048,256]{2,1,0:T(8,128)} async-done(((f32[1,2048,2048]{2,1,0:T(8,128)}), f32[1,2048,256]{2,1,0:T(8,128)}) %reduce-scatter.35.cloned.1.call-update) | async-done | bytes 2097168 | tf_op jit(solution)/shard_map/reduce_scatter | solution.py:180
  2644.1 116.9 %reduce-scatter.33.cloned.1.call-done = f32[1,256,2048]{2,1,0:T(8,128)} async-done(((f32[1,2048,2048]{2,1,0:T(8,128)}), f32[1,256,2048]{2,1,0:T(8,128)}) %reduce-scatter.33.cloned.1.call-update) | async-done | bytes 2097168 | tf_op jit(solution)/shard_map/reduce_scatter | solution.py:179
  2773.1 107.8 %reduce-scatter.37.cloned.1.call-done = f32[1,2048,256]{2,1,0:T(8,128)} async-done(((f32[1,2048,2048]{2,1,0:T(8,128)}), f32[1,2048,256]{2,1,0:T(8,128)}) %reduce-scatter.37.cloned.1.call-update) | async-done | bytes 2097168 | tf_op jit(solution)/shard_map/reduce_scatter | solution.py:180
  (616 shorter events, 751.2 us)
Async XLA Ops:
  11.0 135.7 %all-gather.27.cloned.1.call-start = ((), (), s32[]{:S(2)}) async-start(), calls=%async_computation.28 | async-start | bytes 9437184 | tf_op jit(solution)/shard_map/all_gather | solution.py:167
  12.5 192.4 %all-gather.29.cloned.1.call-start = ((), (), s32[]{:S(2)}) async-start(), calls=%async_computation.29 | async-start | bytes 9437184 | tf_op jit(solution)/shard_map/all_gather | solution.py:168
  15.6 235.6 %all-gather.33.cloned.1.call-start = ((), (), s32[]{:S(2)}) async-start(), calls=%async_computation.31 | async-start | bytes 2359296 | tf_op jit(solution)/shard_map/all_gather | solution.py:166
  16.2 513.3 %all-reduce.20.cloned.1.call-start = ((), (), s32[]{:S(2)}) async-start(), calls=%async_computation.14 | async-start | bytes 16777216 | tf_op jit(solution)/shard_map/psum | solution.py:210
  220.7 355.8 %all-gather.31.cloned.1.call-start = ((), (), s32[]{:S(2)}) async-start(), calls=%async_computation.30 | async-start | bytes 7077888 | tf_op jit(solution)/shard_map/all_gather | solution.py:165
  221.4 501.9 %all-gather.35.cloned.1.call-start = ((), (), s32[]{:S(2)}) async-start(), calls=%async_computation.32 | async-start | bytes 9437184 | tf_op jit(solution)/shard_map/all_gather | solution.py:167
  222.2 535.0 %all-gather.37.cloned.1.call-start = ((), (), s32[]{:S(2)}) async-start(), calls=%async_computation.33 | async-start | bytes 9437184 | tf_op jit(solution)/shard_map/all_gather | solution.py:168
  222.9 885.3 %all-reduce.22.cloned.1.call-start = ((), (), s32[]{:S(2)}) async-start(), calls=%async_computation.15 | async-start | bytes 16777216 | tf_op jit(solution)/shard_map/psum | solution.py:246
  817.2 1023.8 %all-reduce.26.cloned.1.call-start = ((), (), s32[]{:S(2)}) async-start(), calls=%async_computation.39 | async-start | bytes 33554432 | tf_op jit(solution)/shard_map/psum | solution.py:210
  1278.6 598.3 %all-reduce.24.cloned.1.call-start = ((), (), s32[]{:S(2)}) async-start(), calls=%async_computation.38 | async-start | bytes 131072 | tf_op jit(solution)/shard_map/psum | solution.py:246
  1280.6 695.3 %reduce-scatter.45.cloned.1.call-start = ((), (), s32[]{:S(2)}) async-start(), calls=%async_computation.35 | async-start | bytes 73728
  1281.5 695.4 %reduce-scatter.49.cloned.1.call-start = ((), (), s32[]{:S(2)}) async-start(), calls=%async_computation.37 | async-start | bytes 73728
  1282.3 705.2 %reduce-scatter.43.cloned.1.call-start = ((), (), s32[]{:S(2)}) async-start(), calls=%async_computation.34 | async-start | bytes 73728
  1283.1 741.0 %reduce-scatter.47.cloned.1.call-start = ((), (), s32[]{:S(2)}) async-start(), calls=%async_computation.36 | async-start | bytes 73728
  1283.9 795.7 %reduce-scatter.27.cloned.1.call-start = ((), (), s32[]{:S(2)}) async-start(), calls=%async_computation.18 | async-start | bytes 4718592 | tf_op jit(solution)/shard_map/reduce_scatter | solution.py:178
  1290.7 844.1 %reduce-scatter.29.cloned.1.call-start = ((), (), s32[]{:S(2)}) async-start(), calls=%async_computation.19 | async-start | bytes 4718592 | tf_op jit(solution)/shard_map/reduce_scatter | solution.py:178
  1298.7 873.3 %reduce-scatter.39.cloned.1.call-start = ((), (), s32[]{:S(2)}) async-start(), calls=%async_computation.24 | async-start | bytes 73728 | tf_op jit(solution)/shard_map/reduce_scatter | solution.py:183
  1878.4 330.2 %reduce-scatter.41.cloned.1.call-start = ((), (), s32[]{:S(2)}) async-start(), calls=%async_computation.25 | async-start | bytes 73728 | tf_op jit(solution)/shard_map/reduce_scatter | solution.py:183
  1879.9 425.1 %reduce-scatter.23.cloned.1.call-start = ((), (), s32[]{:S(2)}) async-start(), calls=%async_computation.16 | async-start | bytes 14155776 | tf_op jit(solution)/shard_map/reduce_scatter | solution.py:177
  1894.0 507.3 %reduce-scatter.25.cloned.1.call-start = ((), (), s32[]{:S(2)}) async-start(), calls=%async_computation.17 | async-start | bytes 14155776 | tf_op jit(solution)/shard_map/reduce_scatter | solution.py:177
  1910.7 610.6 %reduce-scatter.31.cloned.1.call-start = ((), (), s32[]{:S(2)}) async-start(), calls=%async_computation.20 | async-start | bytes 18874368 | tf_op jit(solution)/shard_map/reduce_scatter | solution.py:179
  1927.2 713.9 %reduce-scatter.35.cloned.1.call-start = ((), (), s32[]{:S(2)}) async-start(), calls=%async_computation.22 | async-start | bytes 18874368 | tf_op jit(solution)/shard_map/reduce_scatter | solution.py:180
  1942.8 818.2 %reduce-scatter.33.cloned.1.call-start = ((), (), s32[]{:S(2)}) async-start(), calls=%async_computation.21 | async-start | bytes 18874368 | tf_op jit(solution)/shard_map/reduce_scatter | solution.py:179
  1959.9 921.0 %reduce-scatter.37.cloned.1.call-start = ((), (), s32[]{:S(2)}) async-start(), calls=%async_computation.23 | async-start | bytes 18874368 | tf_op jit(solution)/shard_map/reduce_scatter | solution.py:180
  (130 other events, 5526.5 us)
Sparse Core Ops, SparseCore 0:
  10.5 48.5 all-gather.22
  92.2 54.3 all-gather.26
  149.0 55.9 all-gather.28
  238.6 290.8 all-reduce.19
  531.9 44.5 all-gather.30
  579.0 54.3 all-gather.34
  635.9 55.9 all-gather.36
  817.4 290.8 all-reduce.21
  1278.8 562.2 all-reduce.25
  1843.9 33.0 all-reduce.23
  1880.8 32.8 reduce-scatter.44
  1917.2 33.2 reduce-scatter.48
  1954.2 33.2 reduce-scatter.42
  1990.9 33.2 reduce-scatter.46
  2028.3 51.3 reduce-scatter.26
  2083.5 51.3 reduce-scatter.28
  2138.7 33.2 reduce-scatter.38
  2175.3 33.2 reduce-scatter.40
  2212.5 92.4 reduce-scatter.22
  2308.9 92.3 reduce-scatter.24
  2405.3 115.9 reduce-scatter.30
  2525.1 115.9 reduce-scatter.34
  2645.1 115.9 reduce-scatter.32
  2764.9 115.9 reduce-scatter.36
  (2 shorter events, 56.5 us)
where the time goes:
time: 2910 us; the launch traced here: 2900 us
  waiting for transfers between devices  2060 us (71%)
  matrix products  430 us (15%)
  local copies, waits for them, and re-layouts  204 us (7%)
  other arithmetic  123 us (4%)
  blocking collectives  55.7 us (2%)
    psum x2, waiting for transfers between devices, layer_forward(): branch = lax.psum(branch, 'mp')  814 us
    psum x2, waiting for transfers between devices, layer_backward(): d_resid, d_norm = lax.psum((d_resid, d_norm), 'mp')  289 us
    reduce_scatter x2, waiting for transfers between devices, reduce_grads(): lax.psum_scatter(grads[2], 'dp', scatter_dimension=1, tiled=True)  227 us
    reduce_scatter x2, waiting for transfers between devices, reduce_grads(): lax.psum_scatter(grads[3], 'dp', scatter_dimension=2, tiled=True)  224 us
    reduce_scatter x2, waiting for transfers between devices, reduce_grads(): lax.psum_scatter(grads[0], 'dp', scatter_dimension=1, tiled=True)  188 us
    reduce_scatter x2, waiting for transfers between devices, reduce_grads(): lax.psum_scatter(grads[1], 'dp', scatter_dimension=2, tiled=True)  108 us
    reduce_scatter x2, waiting for transfers between devices, reduce_grads(): lax.psum_scatter(grads[6], 'dp', scatter_dimension=2, tiled=True)  68.2 us
    dot_general x2, matrix products, layer_forward(): jnp.dot(second_in, up_w, preferred_element_type=jnp.float32)  67.6 us
  transfers between devices with their start and end apart: 26, of which 20 were waited for; matrix products, arithmetic and copies ran while one was open for 17% of the time, Pallas kernels for 0%

commit v1 on v0

--- a/solution.py
+++ b/solution.py
@@ -207,7 +207,9 @@
     branch = jnp.dot(context, dense_w, preferred_element_type=jnp.float32) + jnp.dot(
         active, down_w, preferred_element_type=jnp.float32
     )
-    branch = lax.psum(branch, "mp")
+    branch = branch
+    for hop in (1, 2):
+        branch = branch + lax.ppermute(branch, "mp", [(dev, dev ^ hop) for dev in range(4)])
     result = residual_stream + branch + vec_wide[4] + vec_wide[5]
     return (
         result,

time: 2910 us -> 3300 us (1.13)
  waiting for transfers between devices: 2060 us -> 2420 us
    ppermute x0 -> x4, waiting for transfers between devices: none -> 911 us  [layer_forward(): lax.ppermute(branch, 'mp', [(dev, dev ^ hop) for dev in range(4)])]
    psum x2 -> x0, waiting for transfers between devices: 814 us -> none  [layer_forward(): branch = lax.psum(branch, 'mp')]
    psum x2 -> x3, waiting for transfers between devices: 289 us -> 586 us  [layer_backward(): d_resid, d_norm = lax.psum((d_resid, d_norm), 'mp')]
    all_gather x2, waiting for transfers between devices: 41.5 us -> 4.52 us  [fetch(): lax.all_gather(shards[0][layer], 'dp', axis=0, tiled=True)]
  transfers between devices with their start and end apart: 26 -> 29, of which waited for: 20 -> 22; matrix products, arithmetic and copies ran while one was open for 17% -> 16% of each run, Pallas kernels for 0% -> 0%
where the time goes in v1:
time: 3300 us; the launch traced here: 3290 us
  waiting for transfers between devices  2420 us (73%)
  matrix products  433 us (13%)
  local copies, waits for them, and re-layouts  201 us (6%)
  other arithmetic  153 us (5%)
  blocking collectives  55.4 us (2%)
    ppermute x4, waiting for transfers between devices, layer_forward(): lax.ppermute(branch, 'mp', [(dev, dev ^ hop) for dev in range(4)])  911 us
    psum x3, waiting for transfers between devices, layer_backward(): d_resid, d_norm = lax.psum((d_resid, d_norm), 'mp')  586 us
    reduce_scatter x2, waiting for transfers between devices, reduce_grads(): lax.psum_scatter(grads[2], 'dp', scatter_dimension=1, tiled=True)  227 us
    reduce_scatter x2, waiting for transfers between devices, reduce_grads(): lax.psum_scatter(grads[3], 'dp', scatter_dimension=2, tiled=True)  225 us
    reduce_scatter x2, waiting for transfers between devices, reduce_grads(): lax.psum_scatter(grads[0], 'dp', scatter_dimension=1, tiled=True)  188 us
    reduce_scatter x2, waiting for transfers between devices, reduce_grads(): lax.psum_scatter(grads[1], 'dp', scatter_dimension=2, tiled=True)  108 us
    reduce_scatter x2, waiting for transfers between devices, reduce_grads(): lax.psum_scatter(grads[6], 'dp', scatter_dimension=2, tiled=True)  68.2 us
    dot_general x2, matrix products, layer_forward(): jnp.dot(second_in, up_w, preferred_element_type=jnp.float32)  67.3 us
  transfers between devices with their start and end apart: 29, of which 22 were waited for; matrix products, arithmetic and copies ran while one was open for 16% of the time, Pallas kernels for 0%

profile of v1, /device:TPU:0, one launch (start us, length us, event | category | flops | bytes accessed | tf_op | source)
XLA Modules:
  0.0 3293.9 jit_solution(9075089818109290513)
XLA Ops:
  115.2 31.6 all-gather.27.cloned.1.call-done
  146.8 33.6 %multiply_convert_fusion.4 = (bf16[1024,2048]{1,0:T(8,128)(2,1)}, f32[1024,2048]{1,0:T(8,128)}, f32[1024,2048]{1,0:T(8,128)}) fusion(f32[2048]{0:T(1024)S(1)} %bitcast_convert_fusion.2, bf16[1,2048,2048]{2,1,0:T(8,128)(2,1)} %all-gather.27.cloned.1.call-done, bf16[1024,2048]{1,0:T(8,128)(2,1)} %param.32, f32[2048]{0:T(1024)S(1)} %bitcast.349, ...), kind=kOutput, calls=%fused_computation.189 | convolution fusion | flops 8740929536 | bytes 33587200 | tf_op jit(solution)/shard_map/dot_general | solution.py:203
  180.4 24.7 all-gather.29.cloned.1.call-done
  222.4 181.3 %collective-permute-done = f32[1024,2048]{1,0:T(8,128)} collective-permute-done((f32[1024,2048]{1,0:T(8,128)}, f32[1024,2048]{1,0:T(8,128)}, u32[]{:S(2)}, u32[]{:S(2)}) %collective-permute-start) | collective-permute-done | bytes 8388640 | tf_op jit(solution)/shard_map/ppermute | solution.py:212
  445.9 332.5 %collective-permute-done.1 = f32[1024,2048]{1,0:T(8,128)} collective-permute-done((f32[1024,2048]{1,0:T(8,128)}, f32[1024,2048]{1,0:T(8,128)}, u32[]{:S(2)}, u32[]{:S(2)}) %collective-permute-start.1) | collective-permute-done | bytes 8388640 | tf_op jit(solution)/shard_map/ppermute | solution.py:212
  848.4 33.8 %multiply_convert_fusion.3 = (bf16[1024,2048]{1,0:T(8,128)(2,1)}, f32[1024,2048]{1,0:T(8,128)}, f32[1024,2048]{1,0:T(8,128)}) fusion(f32[2048]{0:T(1024)S(1)} %bitcast_convert_fusion, bf16[1,2048,2048]{2,1,0:T(8,128)(2,1)} %all-gather.35.cloned.1.call-done, f32[1024,2048]{1,0:T(8,128)} %copy-done.1, f32[2048]{0:T(1024)S(1)} %bitcast.353, ...), kind=kOutput, calls=%fused_computation.173 | convolution fusion | flops 8738832384 | bytes 37781504 | tf_op jit(solution)/shard_map/dot_general | solution.py:203
  905.1 174.9 %collective-permute-done.2 = f32[1024,2048]{1,0:T(8,128)} collective-permute-done((f32[1024,2048]{1,0:T(8,128)}, f32[1024,2048]{1,0:T(8,128)}, u32[]{:S(2)}, u32[]{:S(2)}) %collective-permute-start.2) | collective-permute-done | bytes 8388640 | tf_op jit(solution)/shard_map/ppermute | solution.py:212
  1099.1 72.4 %while.54 = (s32[]{:T(128)}, f32[1536,2,256]{0,2,1:T(8,128)}, f32[1536,2,256]{0,2,1:T(8,128)}, f32[2,512,2,256]{1,0,3,2:T(2,128)}, s32[2]{0:T(128)S(1)}, /*index...) while((s32[]{:T(128)}, f32[1536,2,256]{0,2,1:T(8,128)}, ...), condition=%wide.region_18.19_spmd, body=%wide.region_16.18_spmd.sunk | while | flops 2703490560 | bytes 109115848 | solution.py:157
  1232.4 222.8 %collective-permute-done.3 = f32[1024,2048]{1,0:T(8,128)} collective-permute-done((f32[1024,2048]{1,0:T(8,128)}, f32[1024,2048]{1,0:T(8,128)}, u32[]{:S(2)}, u32[]{:S(2)}) %collective-permute-start.3) | collective-permute-done | bytes 8388640 | tf_op jit(solution)/shard_map/ppermute | solution.py:212
  1483.5 291.2 %all-reduce.18.cloned.1.call-done = f32[1024,2048]{1,0:T(8,128)} async-done(((f32[1024,2048]{1,0:T(8,128)}), f32[1024,2048]{1,0:T(8,128)}) %all-reduce.18.cloned.1.call-update) | async-done | bytes 8388624 | tf_op jit(solution)/shard_map/psum | solution.py:248
  1787.5 70.4 %while.55 = (s32[]{:T(128)}, f32[1536,2,256]{0,2,1:T(8,128)}, f32[1536,2,256]{2,0,1:T(8,128)}, f32[2,512,2,256]{3,1,0,2:T(8,128)}, s32[2]{0:T(128)S(1)}, /*index...) while((s32[]{:T(128)}, f32[1536,2,256]{0,2,1:T(8,128)}, ...), condition=%wide.region_24.25_spmd, body=%wide.region_22.24_spmd.sunk | while | flops 2703490560 | bytes 98629992 | solution.py:157
  1964.9 270.0 %all-reduce.20.cloned.1.call-done = f32[1024,2048]{1,0:T(8,128)} async-done(((f32[1024,2048]{1,0:T(8,128)}), f32[1024,2048]{1,0:T(8,128)}) %all-reduce.20.cloned.1.call-update) | async-done | bytes 8388624 | tf_op jit(solution)/shard_map/psum | solution.py:248
  2246.3 24.6 all-reduce.22.cloned.1.call-done
  2384.6 33.4 %reduce-scatter.47.cloned.1.call-done = f32[16,16]{1,0:T(8,128)} async-done(((f32[128,16]{1,0:T(8,128)}), f32[16,16]{1,0:T(8,128)}) %reduce-scatter.47.cloned.1.call-update) | async-done | bytes 1040
  2419.4 54.1 %reduce-scatter.27.cloned.1.call-done = f32[1,512,256]{2,1,0:T(8,128)} async-done(((f32[1,512,2048]{2,1,0:T(8,128)}), f32[1,512,256]{2,1,0:T(8,128)}) %reduce-scatter.27.cloned.1.call-update) | async-done | bytes 524304 | tf_op jit(solution)/shard_map/reduce_scatter | solution.py:178
  2474.7 54.0 %reduce-scatter.29.cloned.1.call-done = f32[1,512,256]{2,1,0:T(8,128)} async-done(((f32[1,512,2048]{2,1,0:T(8,128)}), f32[1,512,256]{2,1,0:T(8,128)}) %reduce-scatter.29.cloned.1.call-update) | async-done | bytes 524304 | tf_op jit(solution)/shard_map/reduce_scatter | solution.py:178
  2533.6 32.0 reduce-scatter.39.cloned.1.call-done
  2566.4 36.1 %reduce-scatter.41.cloned.1.call-done = f32[1,6,256]{2,1,0:T(8,128)} async-done(((f32[1,6,2048]{2,1,0:T(8,128)}), f32[1,6,256]{2,1,0:T(8,128)}) %reduce-scatter.41.cloned.1.call-update) | async-done | bytes 6160 | tf_op jit(solution)/shard_map/reduce_scatter | solution.py:183
  2605.7 93.0 %reduce-scatter.23.cloned.1.call-done = f32[1,256,1536]{2,1,0:T(8,128)} async-done(((f32[1,2048,1536]{2,1,0:T(8,128)}), f32[1,256,1536]{2,1,0:T(8,128)}) %reduce-scatter.23.cloned.1.call-update) | async-done | bytes 1572880 | tf_op jit(solution)/shard_map/reduce_scatter | solution.py:177
  2700.2 94.8 %reduce-scatter.25.cloned.1.call-done = f32[1,256,1536]{2,1,0:T(8,128)} async-done(((f32[1,2048,1536]{2,1,0:T(8,128)}), f32[1,256,1536]{2,1,0:T(8,128)}) %reduce-scatter.25.cloned.1.call-update) | async-done | bytes 1572880 | tf_op jit(solution)/shard_map/reduce_scatter | solution.py:177
  2804.5 110.5 %reduce-scatter.31.cloned.1.call-done = f32[1,256,2048]{2,1,0:T(8,128)} async-done(((f32[1,2048,2048]{2,1,0:T(8,128)}), f32[1,256,2048]{2,1,0:T(8,128)}) %reduce-scatter.31.cloned.1.call-update) | async-done | bytes 2097168 | tf_op jit(solution)/shard_map/reduce_scatter | solution.py:179
  2918.1 116.8 %reduce-scatter.35.cloned.1.call-done = f32[1,2048,256]{2,1,0:T(8,128)} async-done(((f32[1,2048,2048]{2,1,0:T(8,128)}), f32[1,2048,256]{2,1,0:T(8,128)}) %reduce-scatter.35.cloned.1.call-update) | async-done | bytes 2097168 | tf_op jit(solution)/shard_map/reduce_scatter | solution.py:180
  3038.0 116.8 %reduce-scatter.33.cloned.1.call-done = f32[1,256,2048]{2,1,0:T(8,128)} async-done(((f32[1,2048,2048]{2,1,0:T(8,128)}), f32[1,256,2048]{2,1,0:T(8,128)}) %reduce-scatter.33.cloned.1.call-update) | async-done | bytes 2097168 | tf_op jit(solution)/shard_map/reduce_scatter | solution.py:179
  3166.7 108.0 %reduce-scatter.37.cloned.1.call-done = f32[1,2048,256]{2,1,0:T(8,128)} async-done(((f32[1,2048,2048]{2,1,0:T(8,128)}), f32[1,2048,256]{2,1,0:T(8,128)}) %reduce-scatter.37.cloned.1.call-update) | async-done | bytes 2097168 | tf_op jit(solution)/shard_map/reduce_scatter | solution.py:180
  (597 shorter events, 837.8 us)
Async XLA Ops:
  12.5 192.6 %all-gather.29.cloned.1.call-start = ((), (), s32[]{:S(2)}) async-start(), calls=%async_computation.29 | async-start | bytes 9437184 | tf_op jit(solution)/shard_map/all_gather | solution.py:168
  15.6 774.1 %all-gather.31.cloned.1.call-start = ((), (), s32[]{:S(2)}) async-start(), calls=%async_computation.30 | async-start | bytes 7077888 | tf_op jit(solution)/shard_map/all_gather | solution.py:165
  16.2 824.6 %all-gather.33.cloned.1.call-start = ((), (), s32[]{:S(2)}) async-start(), calls=%async_computation.31 | async-start | bytes 2359296 | tf_op jit(solution)/shard_map/all_gather | solution.py:166
  16.7 831.7 %all-gather.35.cloned.1.call-start = ((), (), s32[]{:S(2)}) async-start(), calls=%async_computation.32 | async-start | bytes 9437184 | tf_op jit(solution)/shard_map/all_gather | solution.py:167
  222.3 659.9 %all-gather.37.cloned.1.call-start = ((), (), s32[]{:S(2)}) async-start(), calls=%async_computation.33 | async-start | bytes 9437184 | tf_op jit(solution)/shard_map/all_gather | solution.py:168
  415.6 362.8 %collective-permute-start.1 = (f32[1024,2048]{1,0:T(8,128)}, f32[1024,2048]{1,0:T(8,128)}, u32[]{:S(2)}, u32[]{:S(2)}) collective-permute-start(f32[1024,2048]{1,0:T(8,128)} %add.534), channel_id=1, source_target_pairs={{0,2},{1,3},{2,0},{3,1},{4,6},{5,7},{6,4},{7,5},{8,10},{9,11},{10,... | collective-permute-start | bytes 25165832 | tf_op jit(solution)/shard_map/ppermute | solution.py:212
  418.0 1356.7 %all-reduce.18.cloned.1.call-start = ((), (), s32[]{:S(2)}) async-start(), calls=%async_computation.14 | async-start | bytes 16777216 | tf_op jit(solution)/shard_map/psum | solution.py:248
  1091.9 363.3 %collective-permute-start.3 = (f32[1024,2048]{1,0:T(8,128)}, f32[1024,2048]{1,0:T(8,128)}, u32[]{:S(2)}, u32[]{:S(2)}) collective-permute-start(f32[1024,2048]{1,0:T(8,128)} %add.557), channel_id=1, source_target_pairs={{0,2},{1,3},{2,0},{3,1},{4,6},{5,7},{6,4},{7,5},{8,10},{9,11},{10,... | collective-permute-start | bytes 25165832 | tf_op jit(solution)/shard_map/ppermute | solution.py:212
  1483.4 751.4 %all-reduce.20.cloned.1.call-start = ((), (), s32[]{:S(2)}) async-start(), calls=%async_computation.15 | async-start | bytes 16777216 | tf_op jit(solution)/shard_map/psum | solution.py:248
  1944.8 326.0 %all-reduce.22.cloned.1.call-start = ((), (), s32[]{:S(2)}) async-start(), calls=%async_computation.38 | async-start | bytes 131072 | tf_op jit(solution)/shard_map/psum | solution.py:248
  1946.8 422.8 %reduce-scatter.45.cloned.1.call-start = ((), (), s32[]{:S(2)}) async-start(), calls=%async_computation.35 | async-start | bytes 73728
  1947.7 422.8 %reduce-scatter.49.cloned.1.call-start = ((), (), s32[]{:S(2)}) async-start(), calls=%async_computation.37 | async-start | bytes 73728
  1948.5 432.9 %reduce-scatter.43.cloned.1.call-start = ((), (), s32[]{:S(2)}) async-start(), calls=%async_computation.34 | async-start | bytes 73728
  1949.3 468.7 %reduce-scatter.47.cloned.1.call-start = ((), (), s32[]{:S(2)}) async-start(), calls=%async_computation.36 | async-start | bytes 73728
  1950.1 523.4 %reduce-scatter.27.cloned.1.call-start = ((), (), s32[]{:S(2)}) async-start(), calls=%async_computation.18 | async-start | bytes 4718592 | tf_op jit(solution)/shard_map/reduce_scatter | solution.py:178
  1956.8 571.9 %reduce-scatter.29.cloned.1.call-start = ((), (), s32[]{:S(2)}) async-start(), calls=%async_computation.19 | async-start | bytes 4718592 | tf_op jit(solution)/shard_map/reduce_scatter | solution.py:178
  1964.8 600.8 %reduce-scatter.39.cloned.1.call-start = ((), (), s32[]{:S(2)}) async-start(), calls=%async_computation.24 | async-start | bytes 73728 | tf_op jit(solution)/shard_map/reduce_scatter | solution.py:183
  2272.3 330.2 %reduce-scatter.41.cloned.1.call-start = ((), (), s32[]{:S(2)}) async-start(), calls=%async_computation.25 | async-start | bytes 73728 | tf_op jit(solution)/shard_map/reduce_scatter | solution.py:183
  2273.8 424.9 %reduce-scatter.23.cloned.1.call-start = ((), (), s32[]{:S(2)}) async-start(), calls=%async_computation.16 | async-start | bytes 14155776 | tf_op jit(solution)/shard_map/reduce_scatter | solution.py:177
  2287.9 507.1 %reduce-scatter.25.cloned.1.call-start = ((), (), s32[]{:S(2)}) async-start(), calls=%async_computation.17 | async-start | bytes 14155776 | tf_op jit(solution)/shard_map/reduce_scatter | solution.py:177
  2304.6 610.4 %reduce-scatter.31.cloned.1.call-start = ((), (), s32[]{:S(2)}) async-start(), calls=%async_computation.20 | async-start | bytes 18874368 | tf_op jit(solution)/shard_map/reduce_scatter | solution.py:179
  2321.1 713.8 %reduce-scatter.35.cloned.1.call-start = ((), (), s32[]{:S(2)}) async-start(), calls=%async_computation.22 | async-start | bytes 18874368 | tf_op jit(solution)/shard_map/reduce_scatter | solution.py:180
  2336.6 818.2 %reduce-scatter.33.cloned.1.call-start = ((), (), s32[]{:S(2)}) async-start(), calls=%async_computation.21 | async-start | bytes 18874368 | tf_op jit(solution)/shard_map/reduce_scatter | solution.py:179
  2353.8 921.0 %reduce-scatter.37.cloned.1.call-start = ((), (), s32[]{:S(2)}) async-start(), calls=%async_computation.23 | async-start | bytes 18874368 | tf_op jit(solution)/shard_map/reduce_scatter | solution.py:180
  (120 other events, 10540.1 us)
Sparse Core Ops, SparseCore 0:
  10.5 48.5 all-gather.22
  61.6 28.1 all-gather.24
  92.3 54.4 all-gather.26
  149.1 55.9 all-gather.28
  207.4 45.5 all-gather.30
  286.0 54.3 all-gather.34
  418.1 54.4 all-gather.36
  1483.6 291.0 all-reduce.17
  1945.0 289.8 all-reduce.19
  2237.8 33.0 all-reduce.21
  2274.6 32.8 reduce-scatter.44
  2311.1 33.2 reduce-scatter.48
  2348.1 33.2 reduce-scatter.42
  2384.8 33.2 reduce-scatter.46
  2422.2 51.3 reduce-scatter.26
  2477.3 51.3 reduce-scatter.28
  2532.4 33.2 reduce-scatter.38
  2569.2 33.2 reduce-scatter.40
  2606.2 92.4 reduce-scatter.22
  2702.6 92.3 reduce-scatter.24
  2799.0 115.9 reduce-scatter.30
  2919.0 115.9 reduce-scatter.34
  3038.8 115.9 reduce-scatter.32
  3158.8 115.9 reduce-scatter.36
  (1 shorter events, 28.1 us)
